TPU v7x, 256 devices: a whole 4x4x8 slice. The times are simulated.
256 devices in a mesh: claim: 64 (over y_hi, x, z), feat: 4 (over y_lo, core).
Axes of the slice: x: 4, y: 4 (y_hi: 2, y_lo: 2; y = y_hi * 2 + y_lo), z: 8, core: 2. Of those that a mesh axis runs over, the one named last changes fastest.
Arguments:
- block_tiles: bfloat16 [64, 4, 128, 128, 128], P('claim', 'feat'), may hold values from 0.049804688 to 1
- block_scale: float32 [64, 4, 128], P('claim', 'feat'), may hold values from 1 to 12, as said below
- row_index: int32 [64, 4, 128], P('claim', 'feat'), may hold values from 0 to 63
- col_index: int32 [64, 4, 128], P('claim', 'feat'), may hold values from 0 to 31
- start_basis: float32 [16384, 64], P('feat'), may hold values from -6 to 6
Outputs:
- claim_basis: float32 [524288, 64], P(('claim', 'feat'))
- feature_basis: float32 [16384, 64], P(('feat', 'claim'))
- bidiagonal: float32 [4, 64, 64], replicated
Inputs may be any that keep to these rules, and one draw needn't show every extreme that they name: `row_index`: row block within the device's 64 row blocks of claims; a few row blocks hold most stored blocks. `col_index`: column block within the device's 32 column blocks. `block_scale`: positive block scales.
All inputs are finite; a program needn't handle non-finite values.
Results may differ from a plain program's by a relative error of at most 0.012.
Values may be sent and summed in bfloat16 or wider, within the bound.
A program may use at most 64 MiB of HBM per device.

v0:
```python
import jax
import jax.numpy as jnp
from jax import lax
from jax.sharding import Mesh
from jax.sharding import PartitionSpec as P

BLK_ROWS = 64
HIGH = lax.Precision.HIGHEST
FINE = ("yh", "x", "z", "yl", "c")
CLAIM = ("yh", "x", "z")
FEAT = ("yl", "c")


def forward_local(block_tiles, block_scale, row_index, col_index, operand):
    edge = block_tiles.shape[-1]
    width = operand.shape[-1]
    picked = operand.reshape(-1, edge, width)[col_index]
    products = jnp.einsum("bij,bjk->bik", block_tiles, picked, preferred_element_type=jnp.float32)
    products = products * block_scale[:, None, None]
    selector = (row_index[None, :] == jnp.arange(BLK_ROWS, dtype=jnp.int32)[:, None]).astype(
        jnp.float32
    )
    summed = jnp.einsum("rb,bik->rik", selector, products, precision=HIGH)
    return summed.reshape(BLK_ROWS * edge, width)


def backward_local(block_tiles, block_scale, row_index, col_index, operand, col_count):
    edge = block_tiles.shape[-1]
    width = operand.shape[-1]
    picked = operand.reshape(-1, edge, width)[row_index]
    products = jnp.einsum("bij,bik->bjk", block_tiles, picked, preferred_element_type=jnp.float32)
    products = products * block_scale[:, None, None]
    selector = (col_index[None, :] == jnp.arange(col_count, dtype=jnp.int32)[:, None]).astype(
        jnp.float32
    )
    summed = jnp.einsum("cb,bjk->cjk", selector, products, precision=HIGH)
    return summed.reshape(col_count * edge, width)


def degree_local(block_tiles, block_scale, row_index, col_index, col_count):
    row_sums = jnp.sum(block_tiles, axis=2, dtype=jnp.float32) * block_scale[:, None]
    col_sums = jnp.sum(block_tiles, axis=1, dtype=jnp.float32) * block_scale[:, None]
    row_select = (row_index[None, :] == jnp.arange(BLK_ROWS, dtype=jnp.int32)[:, None]).astype(
        jnp.float32
    )
    col_select = (col_index[None, :] == jnp.arange(col_count, dtype=jnp.int32)[:, None]).astype(
        jnp.float32
    )
    row_part = jnp.einsum("rb,bi->ri", row_select, row_sums, precision=HIGH).reshape(-1)
    col_part = jnp.einsum("cb,bi->ci", col_select, col_sums, precision=HIGH).reshape(-1)
    return (row_part, col_part)


def gram_of(block):
    return jnp.dot(block.T, block, precision=HIGH)


def orthonormal(block, gram_total):
    factor = jnp.linalg.cholesky(gram_total)
    basis = lax.linalg.triangular_solve(
        factor, block, left_side=False, lower=True, transpose_a=True
    )
    return (basis, factor.T)


def claim_sum(value):
    part = lax.psum_scatter(value, "z", scatter_dimension=0, tiled=True)
    part = lax.psum(part, ("yh", "x"))
    return lax.all_gather(part, "z", axis=0, tiled=True)


def all_sum(value):
    value = lax.psum(value, FEAT)
    value = lax.psum(value, "z")
    return lax.psum(value, ("yh", "x"))


def claim_scatter(value):
    size_z = lax.axis_size("z")
    size_o = lax.axis_size("yh") * lax.axis_size("x")
    rows = value.shape[0] // (size_z * size_o)
    blocks = value.reshape(size_o, size_z, rows, -1).transpose(1, 0, 2, 3).reshape(value.shape)
    part = lax.psum_scatter(blocks, "z", scatter_dimension=0, tiled=True)
    return lax.psum_scatter(part, ("yh", "x"), scatter_dimension=0, tiled=True)


def per_device(block_tiles, block_scale, row_index, col_index, start_basis):
    tiles_here = block_tiles.reshape(block_tiles.shape[-3:])
    scale_here = block_scale.reshape(-1)
    rows_here = row_index.reshape(-1)
    cols_here = col_index.reshape(-1)
    edge = tiles_here.shape[-1]
    col_count = start_basis.shape[0] // edge
    claim_count = lax.axis_size(CLAIM)
    own_cols = start_basis.shape[0] // claim_count
    own_first = lax.axis_index(CLAIM) * own_cols
    row_part, col_part = degree_local(tiles_here, scale_here, rows_here, cols_here, col_count)
    col_total = claim_sum(col_part)
    col_scale = lax.rsqrt(col_total + 1.0)
    row_total = lax.psum_scatter(row_part, FEAT, scatter_dimension=0, tiled=True)
    start_total = lax.psum(gram_of(start_basis), FEAT)
    first_basis, _ = orthonormal(start_basis, start_total)
    first_operand = (col_scale[:, None] * first_basis).astype(jnp.bfloat16)
    first_partial = forward_local(tiles_here, scale_here, rows_here, cols_here, first_operand)
    first_sums = lax.psum_scatter(first_partial, FEAT, scatter_dimension=0, tiled=True)
    row_scale = lax.rsqrt(row_total + 1.0)

    def row_orthonormal(block):
        return orthonormal(block, all_sum(gram_of(block)))

    def backward_partial(basis):
        operand = (row_scale[:, None] * basis).astype(jnp.bfloat16)
        gathered = lax.all_gather(operand, FEAT, axis=0, tiled=True)
        return backward_local(tiles_here, scale_here, rows_here, cols_here, gathered, col_count)

    u_first, b_first = row_orthonormal(row_scale[:, None] * first_sums)
    summed = claim_sum(backward_partial(u_first))
    update = col_scale[:, None] * summed - jnp.dot(first_basis, b_first.T, precision=HIGH)
    v_second, a_second = orthonormal(update, lax.psum(gram_of(update), FEAT))
    scaled = (col_scale[:, None] * v_second).astype(jnp.bfloat16)
    second_partial = forward_local(tiles_here, scale_here, rows_here, cols_here, scaled)
    second_sums = lax.psum_scatter(second_partial, FEAT, scatter_dimension=0, tiled=True)
    p_second = row_scale[:, None] * second_sums - jnp.dot(u_first, a_second.T, precision=HIGH)
    u_second, b_second = row_orthonormal(p_second)
    own_sums = claim_scatter(backward_partial(u_second))
    own_scale = lax.dynamic_slice_in_dim(col_scale, own_first, own_cols, 0)
    own_second = lax.dynamic_slice_in_dim(v_second, own_first, own_cols, 0)
    q_second = own_scale[:, None] * own_sums - jnp.dot(own_second, b_second.T, precision=HIGH)
    v_output, a_third = orthonormal(q_second, all_sum(gram_of(q_second)))
    bidiagonal = jnp.stack([b_first, a_second, b_second, a_third])
    return (u_second, v_output, bidiagonal)


def solution(mesh):
    claim_n, feat_n = mesh.devices.shape
    fine = Mesh(mesh.devices.reshape(2, claim_n // 16, 8, 2, feat_n // 2), FINE)
    placed = (
        P(CLAIM, FEAT, None, None, None),
        P(CLAIM, FEAT, None),
        P(CLAIM, FEAT, None),
        P(CLAIM, FEAT, None),
        P(FEAT, None),
    )
    return jax.shard_map(
        per_device,
        mesh=fine,
        in_specs=placed,
        out_specs=(P(CLAIM + FEAT, None), P(FEAT + CLAIM, None), P()),
        check_vma=False,
    )
```

profile of v0, /device:TPU:16, one launch (start us, length us, event | category | flops | bytes accessed | tf_op | source)
XLA Modules:
  0.0 885.8 jit_solution(7263501189897861546)
XLA Ops:
  13.1 32.8 %all-reduce.1 = f32[4096]{0:T(1024)S(1)} all-reduce(f32[4096]{0:T(1024)S(1)} %convolution_bitcast_fusion.5), channel_id=3, replica_groups=mesh['yh'=2,'x'=4,'z'=8,'yl'=2,'c'=2] {'z'}, use_global_device_ids=true, to_apply=%region_3.0.clone | all-reduce | flops 4096 | bytes 32768
  47.2 21.5 %psum.91 = f32[512]{0:T(512)S(1)} all-reduce(f32[512]{0:T(512)S(1)} %dynamic-slice.3), channel_id=1, replica_groups=mesh['yh'=2,'x'=4,'z'=8,'yl'=2,'c'=2] {'yh','x'}, use_global_device_ids=true, to_apply=%region_4.0 | all-reduce | flops 512 | bytes 4096 | tf_op jit(solution)/shard_map/psum | solution.py:68
  68.6 20.8 %all-gather = f32[8,1,512]{2,1,0:T(1,128)S(1)} all-gather(f32[1,1,512]{2,1,0:T(1,128)S(1)} %bitcast.205), channel_id=1, replica_groups=mesh['yh'=2,'x'=4,'z'=8,'yl'=2,'c'=2] {'z'}, dimensions={0}, use_global_device_ids=true | all-gather | bytes 18432 | tf_op jit(solution)/shard_map/all_gather | solution.py:69
  89.7 10.9 %all-reduce.2 = (f32[64,64]{0,1:T(8,128)S(1)}, f32[8192]{0:T(1024)S(1)}) all-reduce(f32[64,64]{0,1:T(8,128)S(1)} %fusion.101, f32[8192]{0:T(1024)S(1)} %convolution_bitcast_fusion.4), channel_id=1, replica_groups=mesh['yh'=2,'x'=4,'z'=8,'yl'=2,'c'=2] {'yl','c'}, use_global_device_ids=true, to_apply=%region_5.0 | all-reduce | flops 12288 | bytes 98304 | tf_op jit(solution)/shard_map/psum | solution.py:101
  100.7 5.8 cholesky.89
  116.2 5.8 multiply_bitcast_fusion.3
  130.0 26.5 %reduce-scatter.6.cloned.1.call-done = f32[2048,64]{0,1:T(8,128)} async-done(((f32[8192,64]{0,1:T(8,128)}), f32[2048,64]{0,1:T(8,128)}) %reduce-scatter.6.cloned.1.call-update) | async-done | bytes 524304 | tf_op jit(solution)/shard_map/reduce_scatter | solution.py:105
  158.4 10.7 %psum.93 = f32[64,64]{0,1:T(8,128)S(1)} all-reduce(f32[64,64]{0,1:T(8,128)S(1)} %fusion.27), channel_id=1, replica_groups=mesh['yh'=2,'x'=4,'z'=8,'yl'=2,'c'=2] {'yl','c'}, use_global_device_ids=true, to_apply=%region_9.12 | all-reduce | flops 4096 | bytes 32768 | tf_op jit(solution)/shard_map/psum | solution.py:73
  169.1 30.2 %psum.94 = f32[64,64]{0,1:T(8,128)S(1)} all-reduce(f32[64,64]{0,1:T(8,128)S(1)} %psum.93), channel_id=1, replica_groups=mesh['yh'=2,'x'=4,'z'=8,'yl'=2,'c'=2] {'z'}, use_global_device_ids=true, to_apply=%region_10.13 | all-reduce | flops 4096 | bytes 32768 | tf_op jit(solution)/shard_map/psum | solution.py:74
  199.3 39.5 %psum.95 = f32[64,64]{0,1:T(8,128)S(1)} all-reduce(f32[64,64]{0,1:T(8,128)S(1)} %psum.94), channel_id=1, replica_groups=mesh['yh'=2,'x'=4,'z'=8,'yl'=2,'c'=2] {'yh','x'}, use_global_device_ids=true, to_apply=%region_11.14 | all-reduce | flops 4096 | bytes 32768 | tf_op jit(solution)/shard_map/psum | solution.py:75
  238.9 5.8 cholesky.100
  246.1 4.9 custom-call.15
  253.6 19.9 %all-gather.5.cloned.1.call-done = bf16[8192,64]{0,1:T(8,128)(2,1)} async-done(((bf16[2048,64]{0,1:T(8,128)(2,1)}), bf16[8192,64]{0,1:T(8,128)(2,1)}) %all-gather.5.cloned.1.call-update) | async-done | bytes 1048592 | tf_op jit(solution)/shard_map/all_gather | solution.py:113
  286.9 40.0 %reduce-scatter.8.cloned.1.call-done = f32[512,64]{0,1:T(8,128)} async-done(((f32[4096,64]{0,1:T(8,128)}), f32[512,64]{0,1:T(8,128)}) %reduce-scatter.8.cloned.1.call-update) | async-done | bytes 131088 | tf_op jit(solution)/shard_map/reduce_scatter | solution.py:67
  327.0 87.9 %all-reduce.5.cloned.1.call-done = f32[512,64]{0,1:T(8,128)} async-done(((f32[512,64]{0,1:T(8,128)}), f32[512,64]{0,1:T(8,128)}) %all-reduce.5.cloned.1.call-update) | async-done | bytes 131088 | tf_op jit(solution)/shard_map/psum | solution.py:68
  414.9 40.9 %all-gather.7.cloned.1.call-done = f32[4096,64]{0,1:T(8,128)} async-done(((f32[512,64]{0,1:T(8,128)}), f32[4096,64]{0,1:T(8,128)}) %all-gather.7.cloned.1.call-update) | async-done | bytes 1048592 | tf_op jit(solution)/shard_map/all_gather | solution.py:69
  459.7 10.7 %psum.97 = f32[64,64]{0,1:T(8,128)S(1)} all-reduce(f32[64,64]{0,1:T(8,128)S(1)} %fusion.102), channel_id=1, replica_groups=mesh['yh'=2,'x'=4,'z'=8,'yl'=2,'c'=2] {'yl','c'}, use_global_device_ids=true, to_apply=%region_14.18 | all-reduce | flops 4096 | bytes 32768 | tf_op jit(solution)/shard_map/psum | solution.py:119
  470.5 5.8 cholesky.111
  487.0 5.8 multiply_bitcast_fusion.1
  499.5 28.9 %reduce-scatter.10.cloned.1.call-done = f32[2048,64]{0,1:T(8,128)} async-done(((f32[8192,64]{0,1:T(8,128)}), f32[2048,64]{0,1:T(8,128)}) %reduce-scatter.10.cloned.1.call-update) | async-done | bytes 524304 | tf_op jit(solution)/shard_map/reduce_scatter | solution.py:122
  531.3 10.7 %psum.98 = f32[64,64]{0,1:T(8,128)S(1)} all-reduce(f32[64,64]{0,1:T(8,128)S(1)} %fusion.103), channel_id=1, replica_groups=mesh['yh'=2,'x'=4,'z'=8,'yl'=2,'c'=2] {'yl','c'}, use_global_device_ids=true, to_apply=%region_16.20 | all-reduce | flops 4096 | bytes 32768 | tf_op jit(solution)/shard_map/psum | solution.py:73
  542.0 30.2 %psum.99 = f32[64,64]{0,1:T(8,128)S(1)} all-reduce(f32[64,64]{0,1:T(8,128)S(1)} %psum.98), channel_id=1, replica_groups=mesh['yh'=2,'x'=4,'z'=8,'yl'=2,'c'=2] {'z'}, use_global_device_ids=true, to_apply=%region_17.21 | all-reduce | flops 4096 | bytes 32768 | tf_op jit(solution)/shard_map/psum | solution.py:74
  572.2 39.5 %psum.100 = f32[64,64]{0,1:T(8,128)S(1)} all-reduce(f32[64,64]{0,1:T(8,128)S(1)} %psum.99), channel_id=1, replica_groups=mesh['yh'=2,'x'=4,'z'=8,'yl'=2,'c'=2] {'yh','x'}, use_global_device_ids=true, to_apply=%region_18.22 | all-reduce | flops 4096 | bytes 32768 | tf_op jit(solution)/shard_map/psum | solution.py:75
  611.8 5.8 cholesky.122
  625.5 19.9 %all-gather.9.cloned.1.call-done = bf16[8192,64]{0,1:T(8,128)(2,1)} async-done(((bf16[2048,64]{0,1:T(8,128)(2,1)}), bf16[8192,64]{0,1:T(8,128)(2,1)}) %all-gather.9.cloned.1.call-update) | async-done | bytes 1048592 | tf_op jit(solution)/shard_map/all_gather | solution.py:113
  653.2 4.9 fusion.8
  662.0 43.3 %reduce-scatter.12.cloned.1.call-done = f32[512,64]{1,0:T(8,128)} async-done(((f32[4096,64]{1,0:T(8,128)}), f32[512,64]{1,0:T(8,128)}) %reduce-scatter.12.cloned.1.call-update) | async-done | bytes 131088 | tf_op jit(solution)/shard_map/reduce_scatter | solution.py:83
  705.4 77.8 %reduce-scatter.14.cloned.1.call-done = f32[64,64]{1,0:T(8,128)} async-done(((f32[512,64]{1,0:T(8,128)}), f32[64,64]{1,0:T(8,128)}) %reduce-scatter.14.cloned.1.call-update) | async-done | bytes 16400 | tf_op jit(solution)/shard_map/reduce_scatter | solution.py:84
  785.2 10.3 %psum.101 = f32[64,64]{0,1:T(8,128)S(1)} all-reduce(f32[64,64]{0,1:T(8,128)S(1)} %fusion.104), channel_id=1, replica_groups=mesh['yh'=2,'x'=4,'z'=8,'yl'=2,'c'=2] {'yl','c'}, use_global_device_ids=true, to_apply=%region_21.25 | all-reduce | flops 4096 | bytes 32768 | tf_op jit(solution)/shard_map/psum | solution.py:73
  795.5 30.2 %psum.102 = f32[64,64]{0,1:T(8,128)S(1)} all-reduce(f32[64,64]{0,1:T(8,128)S(1)} %psum.101), channel_id=1, replica_groups=mesh['yh'=2,'x'=4,'z'=8,'yl'=2,'c'=2] {'z'}, use_global_device_ids=true, to_apply=%region_22.26 | all-reduce | flops 4096 | bytes 32768 | tf_op jit(solution)/shard_map/psum | solution.py:74
  825.7 39.7 %psum.103 = f32[64,64]{0,1:T(8,128)S(1)} all-reduce(f32[64,64]{0,1:T(8,128)S(1)} %psum.102), channel_id=1, replica_groups=mesh['yh'=2,'x'=4,'z'=8,'yl'=2,'c'=2] {'yh','x'}, use_global_device_ids=true, to_apply=%region_23.27 | all-reduce | flops 4096 | bytes 32768 | tf_op jit(solution)/shard_map/psum | solution.py:75
  865.5 5.8 cholesky.133
  (109 shorter events, 96.7 us)
Async XLA Ops:
  7.2 1.3 copy-start
  7.2 38.7 %copy-start.7 = (u32[256]{0:T(256)S(1)}, u32[256]{0:T(256)}, u32[]{:S(2)}) copy-start(u32[256]{0:T(256)} %constant.80) | copy-start | bytes 3076
  7.2 5.7 copy-start.5
  7.2 5.7 copy-start.3
  7.2 82.3 %copy-start.4 = (s32[1,1,128]{2,1,0:T(1,128)S(1)}, s32[1,1,128]{2,1,0:T(1,128)}, u32[]{:S(2)}) copy-start(s32[1,1,128]{2,1,0:T(1,128)} %param.12) | copy-start | bytes 1540
  7.2 149.3 %reduce-scatter.6.cloned.1.call-start = ((), (), s32[]{:S(2)}) async-start(), calls=%async_computation.5 | async-start | bytes 2621440 | tf_op jit(solution)/shard_map/reduce_scatter | solution.py:105
  126.1 2.6 copy-start.6
  128.7 144.8 %all-gather.5.cloned.1.call-start = ((), (), s32[]{:S(2)}) async-start(), calls=%async_computation.6 | async-start | bytes 1310720 | tf_op jit(solution)/shard_map/all_gather | solution.py:113
  253.6 73.4 %reduce-scatter.8.cloned.1.call-start = ((), (), s32[]{:S(2)}) async-start(), calls=%async_computation.7 | async-start | bytes 1179648 | tf_op jit(solution)/shard_map/reduce_scatter | solution.py:67
  286.8 128.0 %all-reduce.5.cloned.1.call-start = ((), (), s32[]{:S(2)}) async-start(), calls=%async_computation.8 | async-start | bytes 262144 | tf_op jit(solution)/shard_map/psum | solution.py:68
  326.9 128.9 %all-gather.7.cloned.1.call-start = ((), (), s32[]{:S(2)}) async-start(), calls=%async_computation.9 | async-start | bytes 1179648 | tf_op jit(solution)/shard_map/all_gather | solution.py:69
  414.9 113.6 %reduce-scatter.10.cloned.1.call-start = ((), (), s32[]{:S(2)}) async-start(), calls=%async_computation.10 | async-start | bytes 2621440 | tf_op jit(solution)/shard_map/reduce_scatter | solution.py:122
  483.7 1.0 copy-start.1
  496.9 31.5 %copy-start.2 = (f32[2048,64]{0,1:T(8,128)S(1)}, f32[2048,64]{0,1:T(8,128)}, u32[]{:S(2)}) copy-start(f32[2048,64]{0,1:T(8,128)} %get-tuple-element.28) | copy-start | bytes 1572868
  499.5 145.9 %all-gather.9.cloned.1.call-start = ((), (), s32[]{:S(2)}) async-start(), calls=%async_computation.11 | async-start | bytes 1310720 | tf_op jit(solution)/shard_map/all_gather | solution.py:113
  625.5 79.8 %reduce-scatter.12.cloned.1.call-start = ((), (), s32[]{:S(2)}) async-start(), calls=%async_computation.12 | async-start | bytes 2359296 | tf_op jit(solution)/shard_map/reduce_scatter | solution.py:83
  662.0 121.3 %reduce-scatter.14.cloned.1.call-start = ((), (), s32[]{:S(2)}) async-start(), calls=%async_computation.13 | async-start | bytes 294912 | tf_op jit(solution)/shard_map/reduce_scatter | solution.py:84
Sparse Core Ops, SparseCore 0:
  128.8 27.6 reduce-scatter.5
  253.7 19.8 all-gather.4
  286.9 39.9 reduce-scatter.7
  329.6 85.2 all-reduce.4
  416.5 39.2 all-gather.6
  499.6 28.7 reduce-scatter.9
  625.6 19.8 all-gather.8
  662.1 43.1 reduce-scatter.11
  709.6 73.5 reduce-scatter.13
where the time goes:
time: 890 us; the launch traced here: 886 us
  waiting for transfers between devices  385 us (43%)
  blocking collectives  338 us (38%)
  other arithmetic  64.9 us (7%)
  matrix products  55.8 us (6%)
  local copies, waits for them, and re-layouts  26.1 us (3%)
  between operations  15.8 us (2%)
    psum x3, blocking collectives, all_sum(): return lax.psum(value, ('yh', 'x'))  119 us
    psum x3, blocking collectives, all_sum(): value = lax.psum(value, 'z')  90.6 us
    psum x1, waiting for transfers between devices, claim_sum(): part = lax.psum(part, ('yh', 'x'))  87.9 us
    reduce_scatter x1, waiting for transfers between devices, claim_scatter(): return lax.psum_scatter(part, ('yh', 'x'), scatter_dimension=0, tiled=True)  77.8 us
    reduce_scatter x1, waiting for transfers between devices, claim_scatter(): part = lax.psum_scatter(blocks, 'z', scatter_dimension=0, tiled=True)  43.3 us
    all_gather x1, waiting for transfers between devices, claim_sum(): return lax.all_gather(part, 'z', axis=0, tiled=True)  40.9 us
    reduce_scatter x1, waiting for transfers between devices, claim_sum(): part = lax.psum_scatter(value, 'z', scatter_dimension=0, tiled=True)  40 us
    all_gather x2, waiting for transfers between devices, backward_partial(): gathered = lax.all_gather(operand, FEAT, axis=0, tiled=True)  39.8 us
  transfers between devices with their start and end apart: 9, of which 9 were waited for; matrix products, arithmetic and copies ran while one was open for 0% of the time, Pallas kernels for 0%

commit v1 on v0

--- a/solution.py
+++ b/solution.py
@@ -9,6 +9,13 @@
 FINE = ("yh", "x", "z", "yl", "c")
 CLAIM = ("yh", "x", "z")
 FEAT = ("yl", "c")
+
+
+def gather_over(x, mesh_axis, dim):
+    size = lax.axis_size(mesh_axis)
+    tiles = jnp.stack([x for _ in range(size)])
+    tiles = lax.all_to_all(tiles, mesh_axis, split_axis=0, concat_axis=0)
+    return jnp.concatenate(tiles, axis=dim)
 
 
 def forward_local(block_tiles, block_scale, row_index, col_index, operand):
@@ -110,7 +117,7 @@
 
     def backward_partial(basis):
         operand = (row_scale[:, None] * basis).astype(jnp.bfloat16)
-        gathered = lax.all_gather(operand, FEAT, axis=0, tiled=True)
+        gathered = gather_over(operand, FEAT, 0)
         return backward_local(tiles_here, scale_here, rows_here, cols_here, gathered, col_count)
 
     u_first, b_first = row_orthonormal(row_scale[:, None] * first_sums)

time: 890 us -> 872 us (0.980)
  waiting for transfers between devices: 385 us -> 350 us
  blocking collectives: 338 us -> 356 us
    all_gather x2 -> x0, waiting for transfers between devices: 39.8 us -> none  [backward_partial(): gathered = lax.all_gather(operand, FEAT, axis=0, tiled=True)]
    all_to_all x0 -> x1, blocking collectives: none -> 17.6 us  [gather_over(): tiles = lax.all_to_all(tiles, mesh_axis, split_axis=0, concat_axis=0)]
    all_to_all x0 -> x1, waiting for transfers between devices: none -> 14.4 us  [gather_over(): tiles = lax.all_to_all(tiles, mesh_axis, split_axis=0, concat_axis=0)]
  transfers between devices with their start and end apart: 9 -> 8, of which waited for: 9 -> 8; matrix products, arithmetic and copies ran while one was open for 0% -> 0% of each run, Pallas kernels for 0% -> 0%
where the time goes in v1:
time: 872 us; the launch traced here: 868 us
  blocking collectives  356 us (41%)
  waiting for transfers between devices  350 us (40%)
  other arithmetic  64.9 us (7%)
  matrix products  53 us (6%)
  local copies, waits for them, and re-layouts  25 us (3%)
  between operations  16.3 us (2%)
    psum x3, blocking collectives, all_sum(): return lax.psum(value, ('yh', 'x'))  119 us
    psum x3, blocking collectives, all_sum(): value = lax.psum(value, 'z')  91 us
    psum x1, waiting for transfers between devices, claim_sum(): part = lax.psum(part, ('yh', 'x'))  88 us
    reduce_scatter x1, waiting for transfers between devices, claim_scatter(): return lax.psum_scatter(part, ('yh', 'x'), scatter_dimension=0, tiled=True)  77.6 us
    all_gather x1, waiting for transfers between devices, claim_sum(): return lax.all_gather(part, 'z', axis=0, tiled=True)  40.9 us
    reduce_scatter x1, waiting for transfers between devices, claim_scatter(): part = lax.psum_scatter(blocks, 'z', scatter_dimension=0, tiled=True)  38.6 us
    reduce_scatter x1, waiting for transfers between devices, claim_sum(): part = lax.psum_scatter(value, 'z', scatter_dimension=0, tiled=True)  35 us
    unnamed x1, blocking collectives  32.8 us
  transfers between devices with their start and end apart: 8, of which 8 were waited for; matrix products, arithmetic and copies ran while one was open for 0% of the time, Pallas kernels for 0%

profile of v1, /device:TPU:16, one launch (start us, length us, event | category | flops | bytes accessed | tf_op | source)
XLA Modules:
  0.0 868.5 jit_solution(9460217736987644725)
XLA Ops:
  13.1 32.8 %all-reduce.1 = f32[4096]{0:T(1024)S(1)} all-reduce(f32[4096]{0:T(1024)S(1)} %convolution_bitcast_fusion.5), channel_id=3, replica_groups=mesh['yh'=2,'x'=4,'z'=8,'yl'=2,'c'=2] {'z'}, use_global_device_ids=true, to_apply=%region_3.0.clone | all-reduce | flops 4096 | bytes 32768
  47.2 21.5 %psum.91 = f32[512]{0:T(512)S(1)} all-reduce(f32[512]{0:T(512)S(1)} %dynamic-slice.3), channel_id=1, replica_groups=mesh['yh'=2,'x'=4,'z'=8,'yl'=2,'c'=2] {'yh','x'}, use_global_device_ids=true, to_apply=%region_4.0 | all-reduce | flops 512 | bytes 4096 | tf_op jit(solution)/shard_map/psum | solution.py:75
  68.6 20.8 %all-gather = f32[8,1,512]{2,1,0:T(1,128)S(1)} all-gather(f32[1,1,512]{2,1,0:T(1,128)S(1)} %bitcast.199), channel_id=1, replica_groups=mesh['yh'=2,'x'=4,'z'=8,'yl'=2,'c'=2] {'z'}, dimensions={0}, use_global_device_ids=true | all-gather | bytes 18432 | tf_op jit(solution)/shard_map/all_gather | solution.py:76
  89.7 10.9 %all-reduce.2 = (f32[64,64]{0,1:T(8,128)S(1)}, f32[8192]{0:T(1024)S(1)}) all-reduce(f32[64,64]{0,1:T(8,128)S(1)} %fusion.101, f32[8192]{0:T(1024)S(1)} %convolution_bitcast_fusion.4), channel_id=1, replica_groups=mesh['yh'=2,'x'=4,'z'=8,'yl'=2,'c'=2] {'yl','c'}, use_global_device_ids=true, to_apply=%region_5.0 | all-reduce | flops 12288 | bytes 98304 | tf_op jit(solution)/shard_map/psum | solution.py:108
  100.7 5.8 cholesky.89
  115.9 5.2 multiply_bitcast_fusion.3
  129.1 26.6 %reduce-scatter.6.cloned.1.call-done = f32[2048,64]{0,1:T(8,128)} async-done(((f32[8192,64]{0,1:T(8,128)}), f32[2048,64]{0,1:T(8,128)}) %reduce-scatter.6.cloned.1.call-update) | async-done | bytes 524304 | tf_op jit(solution)/shard_map/reduce_scatter | solution.py:112
  157.5 10.7 %psum.93 = f32[64,64]{0,1:T(8,128)S(1)} all-reduce(f32[64,64]{0,1:T(8,128)S(1)} %fusion.27), channel_id=1, replica_groups=mesh['yh'=2,'x'=4,'z'=8,'yl'=2,'c'=2] {'yl','c'}, use_global_device_ids=true, to_apply=%region_9.12 | all-reduce | flops 4096 | bytes 32768 | tf_op jit(solution)/shard_map/psum | solution.py:80
  168.2 30.2 %psum.94 = f32[64,64]{0,1:T(8,128)S(1)} all-reduce(f32[64,64]{0,1:T(8,128)S(1)} %psum.93), channel_id=1, replica_groups=mesh['yh'=2,'x'=4,'z'=8,'yl'=2,'c'=2] {'z'}, use_global_device_ids=true, to_apply=%region_10.13 | all-reduce | flops 4096 | bytes 32768 | tf_op jit(solution)/shard_map/psum | solution.py:81
  198.4 39.7 %psum.95 = f32[64,64]{0,1:T(8,128)S(1)} all-reduce(f32[64,64]{0,1:T(8,128)S(1)} %psum.94), channel_id=1, replica_groups=mesh['yh'=2,'x'=4,'z'=8,'yl'=2,'c'=2] {'yh','x'}, use_global_device_ids=true, to_apply=%region_11.14 | all-reduce | flops 4096 | bytes 32768 | tf_op jit(solution)/shard_map/psum | solution.py:82
  238.2 5.8 cholesky.100
  257.5 14.4 %all-to-all-done = bf16[4,2048,64]{1,2,0:T(8,128)(2,1)S(1)} async-done(((bf16[4,2048,64]{1,2,0:T(8,128)(2,1)}), bf16[4,2048,64]{1,2,0:T(8,128)(2,1)S(1)}, u32[]{:S(2)}, u32[]{:S(2)}) %all-to-all-start) | async-done | bytes 1048608 | tf_op jit(solution)/shard_map/all_to_all | solution.py:17
  284.0 35.0 %reduce-scatter.8.cloned.1.call-done = f32[512,64]{0,1:T(8,128)} async-done(((f32[4096,64]{0,1:T(8,128)}), f32[512,64]{0,1:T(8,128)}) %reduce-scatter.8.cloned.1.call-update) | async-done | bytes 131088 | tf_op jit(solution)/shard_map/reduce_scatter | solution.py:74
  319.1 88.0 %all-reduce.5.cloned.1.call-done = f32[512,64]{0,1:T(8,128)} async-done(((f32[512,64]{0,1:T(8,128)}), f32[512,64]{0,1:T(8,128)}) %all-reduce.5.cloned.1.call-update) | async-done | bytes 131088 | tf_op jit(solution)/shard_map/psum | solution.py:75
  407.2 40.9 %all-gather.3.cloned.1.call-done = f32[4096,64]{0,1:T(8,128)} async-done(((f32[512,64]{0,1:T(8,128)}), f32[4096,64]{0,1:T(8,128)}) %all-gather.3.cloned.1.call-update) | async-done | bytes 1048592 | tf_op jit(solution)/shard_map/all_gather | solution.py:76
  452.0 10.5 %psum.97 = f32[64,64]{0,1:T(8,128)S(1)} all-reduce(f32[64,64]{0,1:T(8,128)S(1)} %fusion.102), channel_id=1, replica_groups=mesh['yh'=2,'x'=4,'z'=8,'yl'=2,'c'=2] {'yl','c'}, use_global_device_ids=true, to_apply=%region_14.18 | all-reduce | flops 4096 | bytes 32768 | tf_op jit(solution)/shard_map/psum | solution.py:126
  462.5 5.8 cholesky.111
  477.8 5.2 multiply_bitcast_fusion.1
  489.7 28.9 %reduce-scatter.10.cloned.1.call-done = f32[2048,64]{0,1:T(8,128)} async-done(((f32[8192,64]{0,1:T(8,128)}), f32[2048,64]{0,1:T(8,128)}) %reduce-scatter.10.cloned.1.call-update) | async-done | bytes 524304 | tf_op jit(solution)/shard_map/reduce_scatter | solution.py:129
  521.5 10.7 %psum.98 = f32[64,64]{0,1:T(8,128)S(1)} all-reduce(f32[64,64]{0,1:T(8,128)S(1)} %fusion.103), channel_id=1, replica_groups=mesh['yh'=2,'x'=4,'z'=8,'yl'=2,'c'=2] {'yl','c'}, use_global_device_ids=true, to_apply=%region_16.20 | all-reduce | flops 4096 | bytes 32768 | tf_op jit(solution)/shard_map/psum | solution.py:80
  532.2 30.5 %psum.99 = f32[64,64]{0,1:T(8,128)S(1)} all-reduce(f32[64,64]{0,1:T(8,128)S(1)} %psum.98), channel_id=1, replica_groups=mesh['yh'=2,'x'=4,'z'=8,'yl'=2,'c'=2] {'z'}, use_global_device_ids=true, to_apply=%region_17.21 | all-reduce | flops 4096 | bytes 32768 | tf_op jit(solution)/shard_map/psum | solution.py:81
  562.8 39.2 %psum.100 = f32[64,64]{0,1:T(8,128)S(1)} all-reduce(f32[64,64]{0,1:T(8,128)S(1)} %psum.99), channel_id=1, replica_groups=mesh['yh'=2,'x'=4,'z'=8,'yl'=2,'c'=2] {'yh','x'}, use_global_device_ids=true, to_apply=%region_18.22 | all-reduce | flops 4096 | bytes 32768 | tf_op jit(solution)/shard_map/psum | solution.py:82
  602.0 5.8 cholesky.122
  609.2 4.9 custom-call.17
  615.7 17.6 %all_to_all.10 = bf16[4,2048,64]{1,2,0:T(8,128)(2,1)S(1)} all-to-all(bf16[4,2048,64]{1,2,0:T(8,128)(2,1)S(1)} %stack.30), channel_id=1, replica_groups=mesh['yh'=2,'x'=4,'z'=8,'yl'=2,'c'=2] {'yl','c'}, dimensions={0} | all-to-all | bytes 2097152 | tf_op jit(solution)/shard_map/all_to_all | solution.py:17
  639.9 4.9 fusion.8
  648.8 38.6 %reduce-scatter.12.cloned.1.call-done = f32[512,64]{1,0:T(8,128)} async-done(((f32[4096,64]{1,0:T(8,128)}), f32[512,64]{1,0:T(8,128)}) %reduce-scatter.12.cloned.1.call-update) | async-done | bytes 131088 | tf_op jit(solution)/shard_map/reduce_scatter | solution.py:90
  687.5 77.6 %reduce-scatter.14.cloned.1.call-done = f32[64,64]{1,0:T(8,128)} async-done(((f32[512,64]{1,0:T(8,128)}), f32[64,64]{1,0:T(8,128)}) %reduce-scatter.14.cloned.1.call-update) | async-done | bytes 16400 | tf_op jit(solution)/shard_map/reduce_scatter | solution.py:91
  767.1 10.5 %psum.101 = f32[64,64]{0,1:T(8,128)S(1)} all-reduce(f32[64,64]{0,1:T(8,128)S(1)} %fusion.104), channel_id=1, replica_groups=mesh['yh'=2,'x'=4,'z'=8,'yl'=2,'c'=2] {'yl','c'}, use_global_device_ids=true, to_apply=%region_21.25 | all-reduce | flops 4096 | bytes 32768 | tf_op jit(solution)/shard_map/psum | solution.py:80
  777.7 30.2 %psum.102 = f32[64,64]{0,1:T(8,128)S(1)} all-reduce(f32[64,64]{0,1:T(8,128)S(1)} %psum.101), channel_id=1, replica_groups=mesh['yh'=2,'x'=4,'z'=8,'yl'=2,'c'=2] {'z'}, use_global_device_ids=true, to_apply=%region_22.26 | all-reduce | flops 4096 | bytes 32768 | tf_op jit(solution)/shard_map/psum | solution.py:81
  807.9 39.7 %psum.103 = f32[64,64]{0,1:T(8,128)S(1)} all-reduce(f32[64,64]{0,1:T(8,128)S(1)} %psum.102), channel_id=1, replica_groups=mesh['yh'=2,'x'=4,'z'=8,'yl'=2,'c'=2] {'yh','x'}, use_global_device_ids=true, to_apply=%region_23.27 | all-reduce | flops 4096 | bytes 32768 | tf_op jit(solution)/shard_map/psum | solution.py:82
  847.7 5.8 cholesky.133
  (118 shorter events, 97.4 us)
Async XLA Ops:
  7.2 1.3 copy-start
  7.2 38.7 %copy-start.10 = (u32[256]{0:T(256)S(1)}, u32[256]{0:T(256)}, u32[]{:S(2)}) copy-start(u32[256]{0:T(256)} %constant.80) | copy-start | bytes 3076
  7.2 5.7 copy-start.8
  7.2 5.7 copy-start.6
  7.2 82.3 %copy-start.7 = (s32[1,1,128]{2,1,0:T(1,128)S(1)}, s32[1,1,128]{2,1,0:T(1,128)}, u32[]{:S(2)}) copy-start(s32[1,1,128]{2,1,0:T(1,128)} %param.12) | copy-start | bytes 1540
  7.2 148.5 %reduce-scatter.6.cloned.1.call-start = ((), (), s32[]{:S(2)}) async-start(), calls=%async_computation.7 | async-start | bytes 2621440 | tf_op jit(solution)/shard_map/reduce_scatter | solution.py:112
  113.8 1.0 copy-start.2
  125.3 2.6 copy-start.9
  253.9 18.0 %all-to-all-start = ((bf16[4,2048,64]{1,2,0:T(8,128)(2,1)}), bf16[4,2048,64]{1,2,0:T(8,128)(2,1)S(1)}, u32[]{:S(2)}, u32[]{:S(2)}) async-start(bf16[4,2048,64]{1,2,0:T(8,128)(2,1)} %stack.14), calls=%async_computation.1 | async-start | bytes 2097152 | tf_op jit(solution)/shard_map/all_to_all | solution.py:17
  257.4 61.6 %reduce-scatter.8.cloned.1.call-start = ((), (), s32[]{:S(2)}) async-start(), calls=%async_computation.8 | async-start | bytes 1179648 | tf_op jit(solution)/shard_map/reduce_scatter | solution.py:74
  278.4 169.6 %copy-start.3 = (f32[4096,64]{0,1:T(8,128)S(1)}, f32[4096,64]{0,1:T(8,128)}, u32[]{:S(2)}) copy-start(f32[4096,64]{0,1:T(8,128)} %copy-done.2) | copy-start | bytes 3145732
  284.0 123.1 %all-reduce.5.cloned.1.call-start = ((), (), s32[]{:S(2)}) async-start(), calls=%async_computation.9 | async-start | bytes 262144 | tf_op jit(solution)/shard_map/psum | solution.py:75
  319.0 129.0 %all-gather.3.cloned.1.call-start = ((), (), s32[]{:S(2)}) async-start(), calls=%async_computation.10 | async-start | bytes 1179648 | tf_op jit(solution)/shard_map/all_gather | solution.py:76
  407.1 111.5 %reduce-scatter.10.cloned.1.call-start = ((), (), s32[]{:S(2)}) async-start(), calls=%async_computation.11 | async-start | bytes 2621440 | tf_op jit(solution)/shard_map/reduce_scatter | solution.py:129
  475.7 1.0 copy-start.4
  487.1 31.5 %copy-start.5 = (f32[2048,64]{0,1:T(8,128)S(1)}, f32[2048,64]{0,1:T(8,128)}, u32[]{:S(2)}) copy-start(f32[2048,64]{0,1:T(8,128)} %get-tuple-element.31) | copy-start | bytes 1572868
  489.7 197.7 %reduce-scatter.12.cloned.1.call-start = ((), (), s32[]{:S(2)}) async-start(), calls=%async_computation.12 | async-start | bytes 2359296 | tf_op jit(solution)/shard_map/reduce_scatter | solution.py:90
  644.8 216.6 %copy-start.1 = (f32[4096,64]{0,1:T(8,128)S(1)}, f32[4096,64]{0,1:T(8,128)}, u32[]{:S(2)}) copy-start(f32[4096,64]{0,1:T(8,128)} %param.14) | copy-start | bytes 3145732
  648.8 116.4 %reduce-scatter.14.cloned.1.call-start = ((), (), s32[]{:S(2)}) async-start(), calls=%async_computation.13 | async-start | bytes 294912 | tf_op jit(solution)/shard_map/reduce_scatter | solution.py:91
Sparse Core Ops, SparseCore 0:
  128.0 27.6 reduce-scatter.5
  284.1 34.8 reduce-scatter.7
  321.8 85.2 all-reduce.4
  408.7 39.2 all-gather.2
  489.8 28.7 reduce-scatter.9
  648.9 38.4 reduce-scatter.11
  691.8 73.3 reduce-scatter.13
